TPU v7x, 32 devices: a whole 2x2x4 slice. The times are simulated.
32 devices in a mesh: dp: 16 (over z, x, core), vol: 2 (over y).
Axes of the slice: x: 2, y: 2, z: 4, core: 2. Of those that a mesh axis runs over, the one named last changes fastest.
Arguments:
- images: float32 [32, 128, 128], P(('dp', 'vol')), may hold values from -6 to 6
- contrast: bfloat16 [32, 128, 128], P(('dp', 'vol')), may hold values from -1 to 1
- volume: bfloat16 [256, 256, 256], P('vol'), may hold values from -6 to 6
- line_index: int32 [32, 4, 128], P('dp'), may hold values from 0 to 65278, as said below
- patch_weight: bfloat16 [64, 1024], replicated, may hold values from -0.75 to 0.75
- position: bfloat16 [256, 1024], replicated, may hold values from -3 to 3
- norm_gain: float32 [1024], replicated, may hold values from 0.1 to 1.9
- project_in: bfloat16 [1024, 1536], P('dp'), may hold values from -0.1875 to 0.1875
- project_out: bfloat16 [1024, 512], P('dp'), may hold values from -0.25 to 0.25
- head_weight: float32 [1024, 4], replicated, may hold values from -1.8 to 1.8
Outputs:
- errors: float32 [32, 4], P(('dp', 'vol'))
- in_gradient: float32 [1024, 1536], P('dp')
- out_gradient: float32 [1024, 512], P('dp')
- head_gradient: float32 [1024, 4], replicated
Inputs may be any that keep to these rules, and one draw needn't show every extreme that they name: line_index[i, k, r] = z * 256 + y names the plane z and row y of the volume that row r of hypothesis k of image i samples; z and y lie within 0 and 254.
All inputs are finite; a program needn't handle non-finite values.
Results may differ from a plain program's by a relative error of at most 0.038.
Values may be sent and summed in bfloat16 or wider, within the bound.
A program may use at most 64 MiB of HBM per device.

v0:
```python
import math

import jax
import jax.numpy as jnp
from jax import lax
from jax.sharding import PartitionSpec as P

HEADS = 8
HEAD_DIM = 64
PIX = 128
PATCH = 8
PATCHES = 256
K = 4


EPSILON = 1e-05


def embed_images(images, patch_weight, position):
    count = images.shape[0]
    grid = PIX // PATCH
    pieces = images.reshape(count, grid, PATCH, grid, PATCH).transpose(0, 1, 3, 2, 4)
    pieces = pieces.reshape(count * grid * grid, PATCH * PATCH).astype(jnp.bfloat16)
    mixed = jnp.dot(pieces, patch_weight, preferred_element_type=jnp.float32)
    mixed = mixed.reshape(count, grid * grid, -1) + position.astype(jnp.float32)[None]
    return mixed.reshape(count * grid * grid, -1).astype(jnp.bfloat16)


def normalize(embedded, norm_gain):
    values = embedded.astype(jnp.float32)
    center = values - jnp.mean(values, axis=1, keepdims=True)
    scale = lax.rsqrt(jnp.mean(center * center, axis=1, keepdims=True) + EPSILON)
    return (center * scale * norm_gain[None, :]).astype(jnp.bfloat16)


def attend(triple):
    count = triple.shape[0] // PATCHES
    parts = triple.reshape(count, PATCHES, 3, HEADS, HEAD_DIM).astype(jnp.float32)
    query = parts[:, :, 0]
    keys = parts[:, :, 1]
    values = parts[:, :, 2]
    scores = jnp.einsum("bqhd,bkhd->bhqk", query, keys) * HEAD_DIM ** (-0.5)
    raised = jnp.exp(scores)
    weights = (raised / jnp.sum(raised, axis=-1, keepdims=True)).astype(jnp.bfloat16)
    mixed = jnp.einsum("bhqk,bkhd->bqhd", weights.astype(jnp.float32), values)
    return mixed.reshape(count * PATCHES, HEADS * HEAD_DIM).astype(jnp.bfloat16)


def hartley(images):
    side = images.shape[1]
    freq = jnp.arange(side, dtype=jnp.int32) - side // 2
    place = jnp.arange(side, dtype=jnp.int32)
    phase = (freq[:, None] * place[None, :] % side).astype(jnp.float32) * (2.0 * math.pi / side)
    cosine = jnp.cos(phase)
    sine = jnp.sin(phase)
    highest = lax.Precision.HIGHEST
    first_cos = jnp.einsum("rn,bnm->brm", cosine, images, precision=highest)
    first_sin = jnp.einsum("rn,bnm->brm", sine, images, precision=highest)
    result = jnp.einsum("brm,cm->brc", first_cos, cosine + sine, precision=highest)
    result = result + jnp.einsum("brm,cm->brc", first_sin, cosine - sine, precision=highest)
    return result / side


def render(volume, line_index, slab_index):
    slab, side, _ = volume.shape
    table = volume.reshape(slab * side, side)
    plane = line_index // side - slab_index * slab
    inside = (plane >= 0) & (plane < slab)
    rows = jnp.clip(plane, 0, slab - 1) * side + line_index % side
    picked = jnp.take(table, rows.reshape(-1), axis=0)[:, ::2]
    picked = jnp.where(inside.reshape(-1, 1), picked.astype(jnp.float32), 0.0)
    return (picked.reshape(line_index.shape[0], -1), inside)


def local(
    images,
    contrast,
    volume,
    line_index,
    patch_weight,
    position,
    norm_gain,
    project_in,
    project_out,
    head_weight,
):
    count = images.shape[0]
    width = norm_gain.shape[0]
    highest = lax.Precision.HIGHEST
    rendered, inside = render(volume, line_index, lax.axis_index("vol"))
    spectrum = hartley(images)
    slices = lax.psum_scatter(
        rendered.astype(jnp.bfloat16), "vol", scatter_dimension=0, tiled=True
    ).astype(jnp.float32)
    slices = slices.reshape(count, K, PIX, PIX)
    misfit = contrast.astype(jnp.float32)[:, None] * slices - spectrum[:, None]
    errors = jnp.mean(misfit * misfit, axis=(2, 3))
    embedded = embed_images(images, patch_weight, position)
    normed = normalize(embedded, norm_gain)
    triple = jnp.dot(
        normed,
        lax.all_gather(project_in, "dp", axis=0, tiled=True),
        preferred_element_type=jnp.float32,
    ).astype(jnp.bfloat16)
    attended = attend(triple)
    contract_last = (((1,), (1,)), ((), ()))
    out_whole = lax.all_gather(project_out, "dp", axis=0, tiled=True)
    branch = lax.dot_general(attended, out_whole, contract_last, preferred_element_type=jnp.float32)
    layer_out = embedded.astype(jnp.float32) + branch
    pooled = jnp.mean(layer_out.reshape(count, PATCHES, width), axis=1)
    logits = jnp.dot(pooled, head_weight, precision=highest)
    raised = jnp.exp(logits)
    chances = raised / jnp.sum(raised, axis=1, keepdims=True)
    expected = jnp.sum(chances * errors, axis=1, keepdims=True)
    logit_slope = chances * (errors - expected)
    head_gradient = lax.psum(jnp.dot(pooled.T, logit_slope, precision=highest), ("dp", "vol"))
    pooled_slope = jnp.dot(logit_slope, head_weight.T, precision=highest) / PATCHES
    layer_slope = jnp.broadcast_to(pooled_slope[:, None, :], (count, PATCHES, width))
    layer_slope = layer_slope.reshape(count * PATCHES, width).astype(jnp.bfloat16)
    attended_slope = jnp.dot(layer_slope, out_whole, preferred_element_type=jnp.float32).astype(
        jnp.bfloat16
    )
    triple_slope = jax.vjp(attend, triple)[1](attended_slope)[0]
    contract_first = (((0,), (0,)), ((), ()))
    first = lax.dot_general(
        normed, triple_slope, contract_first, preferred_element_type=jnp.float32
    )
    second = lax.dot_general(
        layer_slope, attended, contract_first, preferred_element_type=jnp.float32
    )
    shard = lax.psum_scatter(
        jnp.concatenate([first, second], axis=1).astype(jnp.bfloat16),
        "dp",
        scatter_dimension=0,
        tiled=True,
    ).astype(jnp.float32)
    shard = lax.psum(shard.astype(jnp.bfloat16), "vol").astype(jnp.float32)
    split = project_in.shape[1]
    return (errors, shard[:, :split], shard[:, split:], head_gradient)


def solution(mesh):
    placed = (
        P(("dp", "vol"), None, None),
        P(("dp", "vol"), None, None),
        P("vol", None, None),
        P("dp", None, None),
        P(),
        P(),
        P(),
        P("dp", None),
        P("dp", None),
        P(),
    )
    return jax.shard_map(
        local,
        mesh=mesh,
        in_specs=placed,
        out_specs=(P(("dp", "vol"), None), P("dp", None), P("dp", None), P()),
        check_vma=False,
    )
```

profile of v0, /device:TPU:0, one launch (start us, length us, event | category | flops | bytes accessed | tf_op | source)
XLA Modules:
  0.0 261.4 jit_solution(18446166115794627641)
XLA Ops:
  8.1 0.7 fusion.38
  9.5 11.4 %gather_fusion = bf16[1024,256]{1,0:T(8,128)(2,1)S(1)} fusion(bf16[32768,256]{1,0:T(8,128)(2,1)} %bitcast.106, s32[1024]{0:T(1024)S(1)} %broadcast_clamp_fusion), kind=kCustom, calls=%fused_computation | custom fusion | bytes 1052672 | tf_op jit(solution)/shard_map/jit(_take)/gather | solution.py:70
  21.2 10.3 %slice.21 = bf16[1024,128]{1,0:T(8,128)(2,1)S(1)} slice(bf16[1024,256]{1,0:T(8,128)(2,1)S(1)} %broadcast_select_fusion), slice={[0:1024:1], [0:256:2]} | slice | bytes 524288 | tf_op jit(solution)/shard_map/slice | solution.py:70
  31.7 0.8 convert_element_type.102
  38.7 19.9 %all-reduce.9.cloned.1.call-done = bf16[2,65536]{1,0:T(2,128)(2,1)} async-done(((bf16[2,65536]{1,0:T(2,128)(2,1)}), bf16[2,65536]{1,0:T(2,128)(2,1)}) %all-reduce.9.cloned.1.call-update) | async-done | bytes 262160
  58.6 1.8 dynamic-slice_convert_fusion
  61.0 22.6 %all-gather.3.cloned.1.call-done = bf16[1024,1536]{1,0:T(8,128)(2,1)} async-done(((bf16[64,1536]{1,0:T(8,128)(2,1)}), bf16[1024,1536]{1,0:T(8,128)(2,1)}) %all-gather.3.cloned.1.call-update) | async-done | bytes 3145744 | tf_op jit(solution)/shard_map/all_gather | solution.py:102
  83.7 3.0 %convolution_convert_fusion.1 = bf16[256,1536]{1,0:T(8,128)(2,1)S(1)} fusion(bf16[1024,1536]{1,0:T(8,128)(2,1)} %all-gather.3.cloned.1.call-done, bf16[256,1024]{1,0:T(8,128)(2,1)S(1)} %get-tuple-element.9, f32[1024]{0:T(1024)S(1)} %copy-done.17, f32[256]{0:T(256)S(1)} %add_rsqrt_fusion, f32[256]{0:T(256)S(1)} %broadcast_multiply_fusion.2), kind=kOutput, calls=%fused_computation.5 | convolution fusion | flops 807010304 | bytes 4462592 | tf_op jit(solution)/shard_map/dot_general | solution.py:100
  88.0 1.2 convolution_convert_fusion.5
  89.3 32.9 %all-gather.5.cloned.1.call-done = bf16[1024,512]{1,0:T(8,128)(2,1)} async-done(((bf16[64,512]{1,0:T(8,128)(2,1)}), bf16[1024,512]{1,0:T(8,128)(2,1)}) %all-gather.5.cloned.1.call-update) | async-done | bytes 1048592 | tf_op jit(solution)/shard_map/all_gather | solution.py:107
  122.2 1.9 fusion.8
  124.2 0.8 fusion.64
  125.0 1.3 multiply_reduce_fusion.1
  126.3 1.2 subtract_multiply_fusion
  128.1 1.5 convolution_convert_fusion.3
  129.6 1.1 convolution_convert_fusion.4
  130.7 1.1 copy.34
  131.8 1.5 fusion.4
  135.6 1.2 convolution_convert_fusion
  136.8 2.6 pad_maximum_fusion
  139.5 71.4 %reduce-scatter.2.cloned.1.call-done = bf16[64,2048]{1,0:T(8,128)(2,1)} async-done(((bf16[1024,2048]{1,0:T(8,128)(2,1)}), bf16[64,2048]{1,0:T(8,128)(2,1)}) %reduce-scatter.2.cloned.1.call-update) | async-done | bytes 262160 | tf_op jit(solution)/shard_map/reduce_scatter | solution.py:131
  211.0 39.6 %psum.15 = f32[1024,4]{0,1:T(4,128)} all-reduce(f32[1024,4]{0,1:T(4,128)S(1)} %broadcast_multiply_fusion), channel_id=1, replica_groups=mesh['dp'=16,'vol'=2] {'dp','vol'}, use_global_device_ids=true, to_apply=%region_11.12 | all-reduce | flops 4096 | bytes 32768 | tf_op jit(solution)/shard_map/psum | solution.py:116
  250.6 1.7 slice.32
  252.3 1.5 slice.33
  (92 shorter events, 12.2 us)
Async XLA Ops:
  8.0 28.7 %copy-start = (bf16[64,1024]{1,0:T(8,128)(2,1)S(1)}, bf16[64,1024]{1,0:T(8,128)(2,1)}, u32[]{:S(2)}) copy-start(bf16[64,1024]{1,0:T(8,128)(2,1)} %param.14) | copy-start | bytes 393220
  8.0 50.5 %all-reduce.9.cloned.1.call-start = ((), (), s32[]{:S(2)}) async-start(), calls=%async_computation.5 | async-start | bytes 524288
  20.9 13.0 %copy-start.7 = (f32[1,128,128]{2,1,0:T(8,128)S(1)}, f32[1,128,128]{2,1,0:T(8,128)}, u32[]{:S(2)}) copy-start(f32[1,128,128]{2,1,0:T(8,128)} %param.10) | copy-start | bytes 196612
  21.0 14.6 %copy-start.8 = (bf16[1,128,128]{2,1,0:T(8,128)(2,1)S(1)}, bf16[1,128,128]{2,1,0:T(8,128)(2,1)}, u32[]{:S(2)}) copy-start(bf16[1,128,128]{2,1,0:T(8,128)(2,1)} %param.11) | copy-start | bytes 98308
  31.5 5.3 %copy-start.6 = (bf16[256,1024]{1,0:T(8,128)(2,1)S(1)}, bf16[256,1024]{1,0:T(8,128)(2,1)}, u32[]{:S(2)}) copy-start(bf16[256,1024]{1,0:T(8,128)(2,1)} %param.15) | copy-start | bytes 1572868
  32.5 51.2 %all-gather.3.cloned.1.call-start = ((), (), s32[]{:S(2)}) async-start(), calls=%async_computation.1 | async-start | bytes 3342336 | tf_op jit(solution)/shard_map/all_gather | solution.py:102
  33.1 89.2 %all-gather.5.cloned.1.call-start = ((), (), s32[]{:S(2)}) async-start(), calls=%async_computation.2 | async-start | bytes 1114112 | tf_op jit(solution)/shard_map/all_gather | solution.py:107
  33.6 177.2 %reduce-scatter.2.cloned.1.call-start = ((), (), s32[]{:S(2)}) async-start(), calls=%async_computation.3 | async-start | bytes 4456448 | tf_op jit(solution)/shard_map/reduce_scatter | solution.py:131
  34.4 3.1 %copy-start.22 = (u32[32]{0:T(128)S(1)}, u32[32]{0:T(128)}, u32[]{:S(2)}) copy-start(u32[32]{0:T(128)} %constant.104) | copy-start | bytes 388
  36.2 47.5 %copy-start.17 = (f32[1024]{0:T(1024)S(1)}, f32[1024]{0:T(1024)}, u32[]{:S(2)}) copy-start(f32[1024]{0:T(1024)} %param.16) | copy-start | bytes 12292
  37.2 49.5 %copy-start.1 = (bf16[256,1024]{1,0:T(8,128)(2,1)}, bf16[256,1024]{1,0:T(8,128)(2,1)S(1)}, u32[]{:S(2)}) copy-start(bf16[256,1024]{1,0:T(8,128)(2,1)S(1)} %get-tuple-element.9) | copy-start | bytes 1572868
  37.2 49.5 %copy-start.12 = (f32[256]{0:T(256)}, f32[256]{0:T(256)S(1)}, u32[]{:S(2)}) copy-start(f32[256]{0:T(256)S(1)} %broadcast_multiply_fusion.2) | copy-start | bytes 3076
  37.5 49.2 %copy-start.19 = (f32[256]{0:T(256)}, f32[256]{0:T(256)S(1)}, u32[]{:S(2)}) copy-start(f32[256]{0:T(256)S(1)} %add_rsqrt_fusion) | copy-start | bytes 3076
  122.2 2.0 copy-start.9
  122.2 2.8 %copy-start.14 = (f32[4]{0:T(128)S(1)}, f32[4]{0:T(128)}, u32[]{:S(2)}) copy-start(f32[4]{0:T(128)} %multiply_reduce_fusion) | copy-start | bytes 52
  122.2 7.4 %copy-start.21 = (bf16[1024,512]{1,0:T(8,128)(2,1)S(1)}, bf16[1024,512]{1,0:T(8,128)(2,1)}, u32[]{:S(2)}) copy-start(bf16[1024,512]{1,0:T(8,128)(2,1)} %all-gather.5.cloned.1.call-done) | copy-start | bytes 3145732
  124.2 3.5 %copy-start.10 = (f32[1024]{0:T(1024)}, f32[1024]{0:T(1024)S(1)}, u32[]{:S(2)}) copy-start(f32[1024]{0:T(1024)S(1)} %broadcast_multiply_fusion.1) | copy-start | bytes 12292
  131.8 1.6 copy-start.4
  134.6 1.0 copy-start.2
  134.6 1.0 copy-start.13
  135.6 1.2 copy-start.5
  139.4 71.5 %copy-start.11 = (f32[1024]{0:T(1024)S(1)}, f32[1024]{0:T(1024)}, u32[]{:S(2)}) copy-start(f32[1024]{0:T(1024)} %copy-done.10) | copy-start | bytes 12292
  139.4 71.5 %copy-start.16 = (f32[4]{0:T(128)S(1)}, f32[4]{0:T(128)}, u32[]{:S(2)}) copy-start(f32[4]{0:T(128)} %copy-done.15) | copy-start | bytes 52
  139.4 111.2 %all-reduce.7.cloned.1.call-start = ((), (), s32[]{:S(2)}) async-start(), calls=%async_computation.4 | async-start | bytes 524288 | tf_op jit(solution)/shard_map/psum | solution.py:137
  (4 other events, 3.6 us)
Sparse Core Ops, SparseCore 0:
  32.6 25.9 all-reduce.8
  211.0 22.3 all-reduce.6
Sparse Core Ops, SparseCore 1:
  35.5 48.1 all-gather.2
  85.9 36.2 all-gather.4
  139.5 71.3 reduce-scatter.1
where the time goes:
time: 262 us; the launch traced here: 261 us
  waiting for transfers between devices  148 us (56%)
  blocking collectives  39.6 us (15%)
  local copies, waits for them, and re-layouts  30.1 us (11%)
  matrix products  17.1 us (7%)
  between operations  16.1 us (6%)
  other arithmetic  10.1 us (4%)
    reduce_scatter x1, waiting for transfers between devices, local(): lax.psum_scatter(jnp.concatenate([first, second], axis=1).astype(jnp.bflo...  71.4 us
    psum x1, blocking collectives, local(): lax.psum(jnp.dot(pooled.T, logit_slope, precision=highest), ('dp', 'vol'))  39.6 us
    all_gather x1, waiting for transfers between devices, local(): out_whole = lax.all_gather(project_out, 'dp', axis=0, tiled=True)  32.9 us
    all_gather x1, waiting for transfers between devices, local(): lax.all_gather(project_in, 'dp', axis=0, tiled=True)  22.6 us
    unnamed x6, waiting for transfers between devices  21 us
    gather x1, local copies, waits for them, and re-layouts, render(): picked = jnp.take(table, rows.reshape(-1), axis=0)[:, ::2]  11.4 us
    slice x1, local copies, waits for them, and re-layouts, render(): picked = jnp.take(table, rows.reshape(-1), axis=0)[:, ::2]  10.3 us
  transfers between devices with their start and end apart: 5, of which 4 were waited for; matrix products, arithmetic and copies ran while one was open for 5% of the time, Pallas kernels for 0%

commit v1 on v0

v1 whole, which is shorter than its diff:
```python
import functools
import math

import jax
import jax.numpy as jnp
import numpy as np
from jax import lax
from jax.experimental import pallas as pl
from jax.experimental.pallas import tpu as pltpu
from jax.sharding import PartitionSpec as P

HEADS = 8
HEAD_DIM = 64
PIX = 128
PATCH = 8
PATCHES = 256
K = 4
EPSILON = 1e-05
F32 = jnp.float32
BF16 = jnp.bfloat16
HIGHEST = lax.Precision.HIGHEST
FIRST = (((0,), (0,)), ((), ()))
LAST = (((1,), (1,)), ((), ()))
MESH = pl.DeviceIdType.MESH


def step(
    dps,
    vols,
    picked,
    patches,
    pieces,
    image,
    contrast,
    patch_weight,
    position,
    gain,
    head_t,
    head_own,
    waves,
    sel,
    errors_out,
    in_out,
    out_out,
    head_out,
    lines,
    patch_buf,
    weight,
    normed,
    attention,
    triple,
    column,
    mean_emb,
    mean_att,
    small_send,
    small_recv,
    total,
    grad_send,
    tile_send,
    grad_recv,
    tile_recv,
    head_send,
    line_sems,
    patch_sems,
    weight_sems,
    small_sems,
    grad_sems,
    tile_sems,
    head_sems,
    local_sems,
):
    dp = lax.axis_index("dp")
    vol = lax.axis_index("vol")
    count = dps * vols
    me = dp * vols + vol
    head = dp % HEADS
    base = dp - head
    rows = weight.shape[1]
    width = gain.shape[1]

    def copy(src, dst, sems, slot_send, slot_recv, to_dp, to_vol):
        return pltpu.make_async_remote_copy(
            src_ref=src,
            dst_ref=dst,
            send_sem=sems.at[0, slot_send],
            recv_sem=sems.at[1, slot_recv],
            device_id=(to_dp, to_vol),
            device_id_type=MESH,
        )

    barrier = pltpu.get_barrier_semaphore()

    def greet(k, c):
        other = (me + k) % count
        pl.semaphore_signal(
            barrier, inc=1, device_id=(other // vols, other % vols), device_id_type=MESH
        )
        return c

    lax.fori_loop(1, count, greet, 0)
    pl.semaphore_wait(barrier, count - 1)

    def patch_copy(k, slot):
        to = base + (head + k) % HEADS
        return copy(patches, patch_buf.at[slot], patch_sems, k, slot, to, vol)

    def weight_copy(k, slot):
        to = (dp + k) % dps
        return copy(pieces.at[to % HEADS], weight.at[slot], weight_sems, k, slot, to, vol)

    def line_copy(k, slot):
        to = (vol + k) % vols
        return copy(picked.at[to], lines.at[slot], line_sems, k, slot, dp, to)

    def each(first, last, body):
        def run(k, c):
            body(k)
            return c

        lax.fori_loop(first, last, run, 0)

    each(1, HEADS, lambda k: patch_copy(k, head).start())
    each(1, dps, lambda k: weight_copy(k, dp).start())
    each(1, vols, lambda k: line_copy(k, vol).start())
    own = [
        pltpu.make_async_copy(patches, patch_buf.at[head], local_sems.at[0]),
        pltpu.make_async_copy(pieces.at[head], weight.at[dp], local_sems.at[1]),
        pltpu.make_async_copy(picked.at[vol], lines.at[vol], local_sems.at[2]),
    ]
    for one in own:
        one.start()

    cosine = waves[0]
    sine = waves[1]
    pixels = image[0]
    first_cos = jnp.dot(cosine, pixels, precision=HIGHEST, preferred_element_type=F32)
    first_sin = jnp.dot(sine, pixels, precision=HIGHEST, preferred_element_type=F32)
    spectrum = jnp.dot(first_cos, waves[2], precision=HIGHEST, preferred_element_type=F32)
    spectrum = spectrum + jnp.dot(
        first_sin, waves[3], precision=HIGHEST, preferred_element_type=F32
    )
    spectrum = spectrum / PIX

    own[0].wait()

    def embed(k, c):
        j = (head + k) % HEADS

        @pl.when(k > 0)
        def _():
            patch_copy(HEADS - k, j).wait_recv()

        pair = patch_buf[j]
        sums = jnp.zeros((1, width), F32)
        for half in range(2):
            part = slice(half * 128, half * 128 + 128)
            values = jnp.dot(
                pair[:, half * 64 : half * 64 + 64],
                patch_weight[...],
                preferred_element_type=F32,
            )
            values = (values + position[part].astype(F32)).astype(BF16).astype(F32)
            sums = sums + jnp.sum(values, axis=0, keepdims=True)
            center = values - jnp.mean(values, axis=1, keepdims=True)
            scale = lax.rsqrt(jnp.mean(center * center, axis=1, keepdims=True) + EPSILON)
            normed[j, part, :] = (center * scale * gain[...]).astype(BF16)
        mean_emb[pl.ds(j, 1), :] = sums / PATCHES
        return c

    lax.fori_loop(0, HEADS, embed, 0)

    own[1].wait()
    each(1, dps, lambda k: weight_copy(k, (dp + dps - k) % dps).wait_recv())

    out_w = weight[:, :, 192:256].reshape(width, HEAD_DIM).astype(F32)
    mixed = jnp.dot(head_t[...], out_w, precision=HIGHEST, preferred_element_type=F32)

    def forward(j, c):
        whole = weight[...].reshape(width, 256)
        t = jnp.dot(normed[j], whole, preferred_element_type=F32).astype(BF16)
        triple[j] = t
        scores = (
            lax.dot_general(t[:, 64:128], t[:, 0:64], LAST, preferred_element_type=F32)
            * HEAD_DIM ** (-0.5)
        )
        raised = jnp.exp(scores)
        chosen = (raised / jnp.sum(raised, axis=0, keepdims=True)).astype(BF16)
        attention[j] = chosen
        col = jnp.sum(chosen.astype(F32), axis=1, keepdims=True)
        column[j] = col
        mean_att[pl.ds(j, 1), :] = (
            jnp.sum(col * t[:, 128:192].astype(F32), axis=0, keepdims=True) / PATCHES
        )
        return c

    lax.fori_loop(0, HEADS, forward, 0)

    own[2].wait()
    each(1, vols, lambda k: line_copy(k, (vol + vols - k) % vols).wait_recv())
    rendered = lines[0].astype(F32)
    for other in range(1, vols):
        rendered = rendered + lines[other].astype(F32)
    slices = jnp.dot(rendered.astype(BF16), sel[...], preferred_element_type=F32)
    lane = lax.broadcasted_iota(jnp.int32, (HEADS, 128), 1)
    row = lax.broadcasted_iota(jnp.int32, (HEADS, 128), 0)
    filt = contrast[0].astype(F32)
    misfits = jnp.zeros((HEADS, 128), F32)
    for k in range(K):
        misfit = filt * slices[k * PIX : (k + 1) * PIX] - spectrum
        value = jnp.sum(jnp.sum(misfit * misfit, axis=0, keepdims=True), axis=1, keepdims=True)
        misfits = jnp.where(lane == k, value / (PIX * PIX), misfits)
    errors_out[...] = misfits
    mine = row == head
    own_emb = jnp.where(
        lax.broadcasted_iota(jnp.int32, (HEADS, width), 0) == head, mean_emb[...], 0.0
    )
    logit = lax.dot_general(
        own_emb, head_t[...], LAST, precision=HIGHEST, preferred_element_type=F32
    )
    logit = logit + lax.dot_general(
        mean_att[...], mixed, LAST, precision=HIGHEST, preferred_element_type=F32
    )
    small_send[0:8, :] = jnp.concatenate([logit, jnp.zeros((HEADS, 120), F32)], axis=1)
    small_send[8:16, :] = jnp.where(mine, misfits, 0.0)

    def small_copy(k, slot):
        to = base + (head + k) % HEADS
        return copy(small_send, small_recv.at[slot], small_sems, k, slot, to, vol)

    each(1, HEADS, lambda k: small_copy(k, head).start())
    small_recv[head] = small_send[...]
    each(1, HEADS, lambda k: small_copy(k, (head + HEADS - k) % HEADS).wait_recv())
    summed = jnp.sum(small_recv[...], axis=0)
    misfits = summed[8:16]
    raised = jnp.where(lane < K, jnp.exp(summed[0:8]), 0.0)
    chances = raised / jnp.sum(raised, axis=1, keepdims=True)
    expected = jnp.sum(chances * misfits, axis=1, keepdims=True)
    slope = chances * (misfits - expected)
    pulled = jnp.zeros((HEADS, HEAD_DIM), F32)
    for k in range(K):
        pulled = pulled + slope[:, k : k + 1] * mixed[k : k + 1, :]
    pulled = pulled / PATCHES
    small_send_slope = slope
    total[...] = jnp.zeros(total.shape, F32)

    for j in range(HEADS):
        t = triple[j]
        chosen = attention[j].astype(F32)
        up = jnp.sum(t[:, 128:192].astype(F32) * pulled[j : j + 1, :], axis=1, keepdims=True)
        center = jnp.sum(chosen * up, axis=0, keepdims=True)
        inner = (chosen * (up - center) * HEAD_DIM ** (-0.5)).astype(BF16)
        key_slope = jnp.dot(inner, t[:, 0:64], preferred_element_type=F32)
        query_slope = lax.dot_general(inner, t[:, 64:128], FIRST, preferred_element_type=F32)
        spread = column[j] * small_send_slope[j : j + 1, :]
        terms = jnp.concatenate([query_slope, key_slope, spread], axis=1).astype(BF16)
        total[...] += lax.dot_general(terms, normed[j], FIRST, preferred_element_type=F32)

    outer = lax.dot_general(
        slope, mean_att[...], FIRST, precision=HIGHEST, preferred_element_type=F32
    )[0:8]
    pooled_t = lax.dot_general(
        jnp.where(mine, slope, 0.0),
        own_emb,
        FIRST,
        precision=HIGHEST,
        preferred_element_type=F32,
    )[0:8]
    pooled_t = pooled_t + lax.dot_general(
        outer, out_w, LAST, precision=HIGHEST, preferred_element_type=F32
    )
    value_t = total[128:136, :]
    for d in range(dps):
        part = slice(d * rows, (d + 1) * rows)
        grad_send[d] = total[0:128, part].T.astype(BF16)
        fill = [jnp.zeros((HEADS, 64 - rows), F32)] if rows < 64 else []
        top = jnp.concatenate([value_t[:, part]] + fill + [outer], axis=1)
        low = jnp.concatenate([mixed] + [pooled_t[:, part]] + fill, axis=1)
        tile_send[d] = jnp.where(row < 4, top, pltpu.roll(low, 4, 0))

    def grad_copy(k, slot):
        to = (me + k) % count
        return copy(
            grad_send.at[to // vols], grad_recv.at[slot], grad_sems, k, slot, to // vols, to % vols
        )

    def tile_copy(k, slot):
        to = (me + k) % count
        return copy(
            tile_send.at[to // vols], tile_recv.at[slot], tile_sems, k, slot, to // vols, to % vols
        )

    each(1, count, lambda k: tile_copy(k, me).start())
    each(1, count, lambda k: grad_copy(k, me).start())
    grad_recv[me] = grad_send[dp]
    tile_recv[me] = tile_send[dp]
    each(1, count, lambda k: tile_copy(k, (me + count - k) % count).wait_recv())

    pooled_sum = jnp.sum(tile_recv[...], axis=0)
    head_send[...] = pooled_sum

    def head_copy(k, slot):
        to = (dp + k) % dps
        return copy(head_send, head_out.at[slot], head_sems, k, slot, to, vol)

    each(1, dps, lambda k: head_copy(k, dp).start())
    head_out[dp] = pooled_sum

    for h in range(HEADS):
        senders = [
            (d * vols + v) for d in range(h, dps, HEADS) for v in range(vols)
        ]
        tile = tile_recv[senders[0]]
        mixed_h = jnp.where(row < 4, pltpu.roll(tile, 4, 0), 0.0)[:, 0:64]
        for s in senders[1:]:
            tile = tile + tile_recv[s]
        tile = jnp.where(row < 4, tile, 0.0)
        lanes = slice(h * 64, h * 64 + 64)
        in_out[:, 1024 + h * 64 : 1088 + h * 64] = (
            lax.dot_general(
                tile[:, 0:rows], mixed_h, FIRST, precision=HIGHEST, preferred_element_type=F32
            )
            / PATCHES
        )
        out_out[:, lanes] = lax.dot_general(
            head_own[...], tile[:, 64:128], FIRST, precision=HIGHEST, preferred_element_type=F32
        )
    each(1, count, lambda k: grad_copy(k, (me + count - k) % count).wait_recv())
    for h in range(HEADS):
        senders = [
            (d * vols + v) for d in range(h, dps, HEADS) for v in range(vols)
        ]
        both = grad_recv[senders[0]].astype(F32)
        for s in senders[1:]:
            both = both + grad_recv[s].astype(F32)
        in_out[:, h * 64 : h * 64 + 64] = both[:, 0:64]
        in_out[:, 512 + h * 64 : 576 + h * 64] = both[:, 64:128]
    each(1, dps, lambda k: head_copy(k, (dp + dps - k) % dps).wait_recv())

    each(1, HEADS, lambda k: patch_copy(k, head).wait_send())
    each(1, dps, lambda k: weight_copy(k, dp).wait_send())
    each(1, vols, lambda k: line_copy(k, vol).wait_send())
    each(1, HEADS, lambda k: small_copy(k, head).wait_send())
    each(1, count, lambda k: tile_copy(k, me).wait_send())
    each(1, count, lambda k: grad_copy(k, me).wait_send())
    each(1, dps, lambda k: head_copy(k, dp).wait_send())


def constants():
    freq = np.arange(PIX) - PIX // 2
    phase = (freq[:, None] * np.arange(PIX)[None, :] % PIX) * (2.0 * math.pi / PIX)
    cosine, sine = np.cos(phase), np.sin(phase)
    waves = np.stack([cosine, sine, (cosine + sine).T, (cosine - sine).T]).astype(np.float32)
    sel = np.zeros((2 * PIX, PIX), np.float32)
    sel[2 * np.arange(PIX), np.arange(PIX)] = 1.0
    return waves, sel


def local(
    dps,
    vols,
    images,
    contrast,
    volume,
    line_index,
    patch_weight,
    position,
    norm_gain,
    project_in,
    project_out,
    head_weight,
):
    width = norm_gain.shape[0]
    rows = project_in.shape[0]
    count = dps * vols
    waves, sel = constants()
    slab, side, _ = volume.shape
    plane = line_index // side - lax.axis_index("vol") * slab
    inside = (plane >= 0) & (plane < slab)
    spot = jnp.clip(plane, 0, slab - 1) * side + line_index % side
    picked = jnp.take(volume.reshape(slab * side, side), spot.reshape(-1), axis=0)
    picked = jnp.where(inside.reshape(-1, 1), picked, jnp.zeros((), BF16))
    picked = picked.reshape(vols, K * PIX, side)

    grid = PIX // PATCH
    patches = images[0].astype(BF16).reshape(2, grid // 2, PATCH, grid, PATCH)
    patches = patches.transpose(1, 3, 0, 2, 4).reshape(PATCHES // 2, 2 * PATCH * PATCH)
    parts = project_in.reshape(rows, 3, HEADS, HEAD_DIM).transpose(2, 0, 1, 3)
    pieces = jnp.concatenate(
        [parts, project_out.reshape(rows, HEADS, 1, HEAD_DIM).transpose(1, 0, 2, 3)], axis=2
    ).reshape(HEADS, rows, 4 * HEAD_DIM)
    head_t = jnp.pad(head_weight.T, ((0, 4), (0, 0)))
    head_own = lax.dynamic_slice(head_t, (0, lax.axis_index("dp") * rows), (8, rows))

    vmem = pl.BlockSpec(memory_space=pltpu.VMEM)
    errors, in_grad, out_grad, head_grad = pl.pallas_call(
        functools.partial(step, dps, vols),
        out_shape=(
            jax.ShapeDtypeStruct((8, 128), F32),
            jax.ShapeDtypeStruct((rows, 3 * HEADS * HEAD_DIM), F32),
            jax.ShapeDtypeStruct((rows, HEADS * HEAD_DIM), F32),
            jax.ShapeDtypeStruct((dps, 8, 128), F32),
        ),
        in_specs=[vmem] * 12,
        out_specs=(vmem,) * 4,
        scratch_shapes=[
            pltpu.VMEM((vols, K * PIX, side), BF16),
            pltpu.VMEM((HEADS, PATCHES // 2, 128), BF16),
            pltpu.VMEM((dps, rows, 256), BF16),
            pltpu.VMEM((HEADS, PATCHES, width), BF16),
            pltpu.VMEM((HEADS, PATCHES, PATCHES), BF16),
            pltpu.VMEM((HEADS, PATCHES, 256), BF16),
            pltpu.VMEM((HEADS, PATCHES, 1), F32),
            pltpu.VMEM((HEADS, width), F32),
            pltpu.VMEM((HEADS, HEAD_DIM), F32),
            pltpu.VMEM((16, 128), F32),
            pltpu.VMEM((HEADS, 16, 128), F32),
            pltpu.VMEM((256, width), F32),
            pltpu.VMEM((dps, rows, 128), BF16),
            pltpu.VMEM((dps, 8, 128), F32),
            pltpu.VMEM((count, rows, 128), BF16),
            pltpu.VMEM((count, 8, 128), F32),
            pltpu.VMEM((8, 128), F32),
            pltpu.SemaphoreType.DMA((2, vols)),
            pltpu.SemaphoreType.DMA((2, HEADS)),
            pltpu.SemaphoreType.DMA((2, dps)),
            pltpu.SemaphoreType.DMA((2, HEADS)),
            pltpu.SemaphoreType.DMA((2, count)),
            pltpu.SemaphoreType.DMA((2, count)),
            pltpu.SemaphoreType.DMA((2, dps)),
            pltpu.SemaphoreType.DMA((3,)),
        ],
        compiler_params=pltpu.CompilerParams(
            collective_id=0, has_side_effects=True, vmem_limit_bytes=56 * 1024 * 1024
        ),
        name="pose_step",
    )(
        picked,
        patches,
        pieces,
        images,
        contrast,
        patch_weight,
        position,
        norm_gain.reshape(1, width),
        head_t,
        head_own,
        jnp.asarray(waves),
        jnp.asarray(sel, BF16),
    )
    head_grad = head_grad[:, 4:8, 64 : 64 + rows].transpose(0, 2, 1).reshape(width, 4)
    return errors[0:1, 0:K], in_grad, out_grad, head_grad


def solution(mesh):
    placed = (
        P(("dp", "vol"), None, None),
        P(("dp", "vol"), None, None),
        P("vol", None, None),
        P("dp", None, None),
        P(),
        P(),
        P(),
        P("dp", None),
        P("dp", None),
        P(),
    )
    return jax.shard_map(
        functools.partial(local, mesh.shape["dp"], mesh.shape["vol"]),
        mesh=mesh,
        in_specs=placed,
        out_specs=(P(("dp", "vol"), None), P("dp", None), P("dp", None), P()),
        check_vma=False,
    )
```

time: 262 us -> 90.1 us (0.34)
  waiting for transfers between devices: 148 us -> 0 us
  Pallas kernels: 0 us -> 58.2 us
  blocking collectives: 39.6 us -> 0 us
  matrix products: 17.1 us -> 0 us
  between operations: 16.1 us -> 0.75 us
  other arithmetic: 10.1 us -> 4.78 us
  local copies, waits for them, and re-layouts: 30.1 us -> 25.8 us
    reduce_scatter x1 -> x0, waiting for transfers between devices: 71.4 us -> none  [local(): lax.psum_scatter(jnp.concatenate([first, second], axis=1).astype(jnp.bflo...]
    pallas_call x0 -> x1, Pallas kernels: none -> 58.2 us  [local(): pl.pallas_call(functools.partial(step, dps, vols), out_shape=(jax.ShapeDt...]
    all_gather x2 -> x0, waiting for transfers between devices: 55.5 us -> none  [the longest x1 32.9 us: local(): out_whole = lax.all_gather(project_out, 'dp', axis=0, tiled=True)]
    psum x1 -> x0, blocking collectives: 39.6 us -> none  [local(): lax.psum(jnp.dot(pooled.T, logit_slope, precision=highest), ('dp', 'vol'))]
    unnamed x6 -> x0, waiting for transfers between devices: 21 us -> none
    dot_general x18 -> x0, matrix products: 17.1 us -> none  [the longest x3 3.2 us: attend(): mixed = jnp.einsum('bhqk,bkhd->bqhd', weights.astype(jnp.float32), values)]
    slice x3 -> x1, local copies, waits for them, and re-layouts: 13.5 us -> 1.19 us  [local(): return (errors[0:1, 0:K], in_grad, out_grad, head_grad)]
    reshape x0 -> x8, local copies, waits for them, and re-layouts: none -> 5.23 us  [the longest x2 1.39 us: local(): parts = project_in.reshape(rows, 3, HEADS, HEAD_DIM).transpose(2, 0, 1, 3)]
  transfers between devices with their start and end apart: 5 -> 0, of which waited for: 4 -> 0; matrix products, arithmetic and copies ran while one was open for 5% -> 0% of each run, Pallas kernels for 0% -> 0%
where the time goes in v1:
time: 90.1 us; the launch traced here: 89.5 us
  Pallas kernels  58.2 us (65%)
  local copies, waits for them, and re-layouts  25.8 us (29%)
  other arithmetic  4.78 us (5%)
    pallas_call x1, Pallas kernels, local(): pl.pallas_call(functools.partial(step, dps, vols), out_shape=(jax.ShapeDt...  58.2 us
    gather x1, local copies, waits for them, and re-layouts, local(): jnp.take(volume.reshape(slab * side, side), spot.reshape(-1), axis=0)  11.6 us
    unnamed x3, local copies, waits for them, and re-layouts  3.34 us

profile of v1, /device:TPU:0, one launch (start us, length us, event | category | flops | bytes accessed | tf_op | source)
XLA Modules:
  0.0 89.5 jit_solution(571526723568006794)
XLA Ops:
  0.6 0.7 and_bitcast_fusion
  1.4 1.4 %pad_dynamic-slice_fusion.head_own = f32[8,64]{1,0:T(8,128)} fusion(s32[]{:T(128)S(6)} %select_n.48, f32[4,1024]{1,0:T(4,128)} %bitcast.35), kind=kLoop, calls=%fused_computation.10 | loop fusion | bytes 18436 | tf_op jit(solution)/shard_map/dynamic_slice | solution.py:392
  2.7 0.7 fusion.3
  3.4 0.7 fusion.1
  4.2 1.3 %pad.4.head_t = f32[8,1024]{1,0:T(8,128)} pad(f32[4,1024]{1,0:T(4,128)} %bitcast.36, f32[]{:T(128)} %constant.67.clone.1), padding=0_4x0_0 | pad | bytes 49156 | tf_op jit(solution)/shard_map/jit(_pad)/pad | solution.py:391
  5.5 0.8 convert_element_type.9
  6.3 1.0 %reshape.90 = bf16[64,8,1,64]{3,1,0,2:T(8,128)(2,1)S(1)} reshape(bf16[64,512]{1,0:T(8,128)(2,1)} %param.20) | data formatting | bytes 131072 | tf_op jit(solution)/shard_map/reshape | solution.py:389
  7.3 0.2 copy.31
  7.5 1.2 %reshape.89 = bf16[64,3,8,64]{3,2,1,0:T(8,128)(2,1)S(1)} reshape(bf16[64,1536]{1,0:T(8,128)(2,1)} %param.19) | data formatting | bytes 393216 | tf_op jit(solution)/shard_map/reshape | solution.py:387
  8.7 0.2 copy.30
  8.9 0.7 pad_maximum_fusion
  9.6 1.0 %reshape.91.pieces = bf16[8,64,256]{2,1,0:T(8,128)(2,1)} reshape(bf16[8,64,4,64]{3,2,1,0:T(4,128)(2,1)S(1)} %pad_maximum_fusion) | data formatting | bytes 524288 | tf_op jit(solution)/shard_map/reshape | solution.py:390
  10.7 0.6 convert_element_type.10
  11.3 0.3 copy.19
  11.5 0.2 reshape.88
  11.7 0.7 copy.22.patches
  12.5 11.6 %gather_fusion = bf16[1024,256]{1,0:T(8,128)(2,1)S(1)} fusion(bf16[32768,256]{1,0:T(8,128)(2,1)} %bitcast.34, s32[1024]{0:T(1024)S(1)} %broadcast_clamp_fusion), kind=kCustom, calls=%fused_computation | custom fusion | bytes 1052672 | tf_op jit(solution)/shard_map/jit(_take)/gather | solution.py:380
  24.0 1.1 %select_select_fusion.picked = bf16[2,512,256]{2,1,0:T(8,128)(2,1)} fusion(bf16[2,512,256]{2,1,0:T(8,128)(2,1)S(1)} %bitcast.32, pred[2,512]{1,0:T(4,128)(4,1)S(1)} %compare_and_fusion, pred[2,512]{1,0:T(4,128)(4,1)S(1)} %bitcast.39), kind=kLoop, calls=%fused_computation.3 | loop fusion | flops 524288 | bytes 1050624 | tf_op jit(solution)/shard_map/jit(_where)/select_n | solution.py:381
  25.2 58.2 %pose_step.1 = (f32[8,128]{1,0:T(8,128)}, f32[64,1536]{1,0:T(8,128)}, f32[64,512]{1,0:T(8,128)}, f32[16,8,128]{2,1,0:T(8,128)}) custom-call(bf16[2,512,256]{2,1,0:T(8,128)(2,1)} %select_select_fusion.picked, bf16[128,128]{1,0:T(8,128)(2,1)} %copy.22.patches, bf16[8,64,256]{2,1,0:T(8,128)(2,1)} %reshape.91.pieces, f32[1,128,128]{2,1,0:T(8,128)} %image.1, ...), custom_call_target="tpu_custom_call" | custom-call | tf_op jit(solution)/shard_map/pose_step/pallas_call | solution.py:395
  83.4 1.2 %slice.6 = f32[1,4]{1,0:T(1,128)} slice(f32[8,128]{1,0:T(8,128)} %get-tuple-element.8), slice={[0:1], [0:4]} | slice | bytes 32 | tf_op jit(solution)/shard_map/slice | solution.py:451
  84.5 0.9 %slice_bitcast_fusion = f32[16,64,4]{1,2,0:T(4,128)S(1)} fusion(f32[16,8,128]{2,1,0:T(8,128)} %get-tuple-element.11), kind=kLoop, calls=%fused_computation.5 | loop fusion | bytes 32768 | tf_op jit(solution)/shard_map/transpose | solution.py:450
  85.5 0.7 reshape.93
  86.2 1.8 %copy.35 = f32[64,1536]{1,0:T(8,128)} copy(f32[64,1536]{1,0:T(8,128)} %get-tuple-element.17) | data formatting | bytes 786432
  87.9 1.6 %copy.36 = f32[64,512]{1,0:T(8,128)} copy(f32[64,512]{1,0:T(8,128)} %get-tuple-element.18) | data formatting | bytes 262144
  (5 shorter events, 0.0 us)

commit v2 on v1

--- a/solution.py
+++ b/solution.py
@@ -27,22 +27,30 @@
 def step(
     dps,
     vols,
-    picked,
-    patches,
-    pieces,
+    spots,
+    index,
+    volume,
     image,
     contrast,
     patch_weight,
     position,
     gain,
-    head_t,
-    head_own,
+    project_in,
+    project_out,
+    head_weight,
     waves,
     sel,
+    places,
     errors_out,
-    in_out,
-    out_out,
+    grad_recv,
+    value_out,
     head_out,
+    slab_buf,
+    picked,
+    patches,
+    pieces,
+    head_wide,
+    terms_buf,
     lines,
     patch_buf,
     weight,
@@ -54,10 +62,11 @@
     mean_att,
     small_send,
     small_recv,
-    total,
+    pulled_buf,
+    slope_buf,
+    pooled_buf,
     grad_send,
     tile_send,
-    grad_recv,
     tile_recv,
     head_send,
     line_sems,
@@ -77,6 +86,9 @@
     base = dp - head
     rows = weight.shape[1]
     width = gain.shape[1]
+    slab = volume.shape[0]
+    load = pltpu.make_async_copy(volume, slab_buf, local_sems.at[2])
+    load.start()
 
     def copy(src, dst, sems, slot_send, slot_recv, to_dp, to_vol):
         return pltpu.make_async_remote_copy(
@@ -98,6 +110,21 @@
         return c
 
     lax.fori_loop(1, count, greet, 0)
+    for h in range(HEADS):
+        pieces[h] = jnp.concatenate(
+            [project_in[:, p * 512 + h * 64 : p * 512 + h * 64 + 64] for p in range(3)]
+            + [project_out[:, h * 64 : h * 64 + 64]],
+            axis=1,
+        )
+    cells = lax.broadcasted_iota(jnp.int32, (16, 16, 128), 1)
+    spread_lane = lax.broadcasted_iota(jnp.int32, (16, 16, 128), 2)
+    cut = jnp.zeros((PATCHES, 128), F32)
+    for r in range(PATCH):
+        stripe = image[0, pl.ds(r, 16, stride=PATCH), :]
+        stripe = jnp.broadcast_to(stripe[:, None, :], (16, 16, 128))
+        stripe = jnp.where(spread_lane // PATCH == cells, stripe, 0.0).reshape(PATCHES, 128)
+        cut = cut + jnp.dot(stripe.astype(BF16), places[r], preferred_element_type=F32)
+    patches[...] = jnp.concatenate([cut[0:128, 0:64], cut[128:256, 0:64]], axis=1).astype(BF16)
     pl.semaphore_wait(barrier, count - 1)
 
     def patch_copy(k, slot):
@@ -110,7 +137,7 @@
 
     def line_copy(k, slot):
         to = (vol + k) % vols
-        return copy(picked.at[to], lines.at[slot], line_sems, k, slot, dp, to)
+        return copy(picked.at[k], lines.at[slot], line_sems, k, slot, dp, to)
 
     def each(first, last, body):
         def run(k, c):
@@ -121,11 +148,9 @@
 
     each(1, HEADS, lambda k: patch_copy(k, head).start())
     each(1, dps, lambda k: weight_copy(k, dp).start())
-    each(1, vols, lambda k: line_copy(k, vol).start())
     own = [
         pltpu.make_async_copy(patches, patch_buf.at[head], local_sems.at[0]),
         pltpu.make_async_copy(pieces.at[head], weight.at[dp], local_sems.at[1]),
-        pltpu.make_async_copy(picked.at[vol], lines.at[vol], local_sems.at[2]),
     ]
     for one in own:
         one.start()
@@ -140,6 +165,9 @@
         first_sin, waves[3], precision=HIGHEST, preferred_element_type=F32
     )
     spectrum = spectrum / PIX
+
+    head_wide[...] = jnp.concatenate([head_weight[...], jnp.zeros((width, 124), F32)], axis=1)
+    head_t = head_wide[...].T[0:8]
 
     own[0].wait()
 
@@ -167,13 +195,53 @@
         mean_emb[pl.ds(j, 1), :] = sums / PATCHES
         return c
 
+    load.wait()
+
+    def render(step_k, c):
+        k = step_k + 1
+        v = (vol + k) % vols
+        turned = jnp.concatenate([index[v], jnp.zeros((4, 128), jnp.int32)], axis=0)
+        turned = turned.astype(F32).T.astype(jnp.int32)
+        spot_lane = lax.broadcasted_iota(jnp.int32, (128, 256), 1)
+        spot_row = lax.broadcasted_iota(jnp.int32, (128, 256), 0)
+        for hyp in range(K):
+            line = turned[:, hyp : hyp + 1]
+            level = (line >> 8) - vol * slab
+            target = jnp.where((level >= 0) & (level < slab), line & 15, 1024)
+            hot = jnp.where(spot_lane == (spot_row % 16) * 16 + target, 1.0, 0.0).astype(BF16)
+            found = []
+            for group in range(8):
+                tiles = []
+                for i in range(16):
+                    spot = spots[v, hyp, group * 16 + i]
+                    level = jnp.clip((spot >> 8) - vol * slab, 0, slab - 1)
+                    tiles.append(slab_buf[level, (spot >> 4) & 15])
+                tiles = jnp.concatenate(tiles, axis=0)
+                found.append(
+                    jnp.dot(
+                        hot[group * 16 : group * 16 + 16], tiles, preferred_element_type=F32
+                    )
+                )
+            found = jnp.concatenate(found, axis=0).astype(BF16)
+            picked[k, hyp * PIX : (hyp + 1) * PIX, :] = jnp.dot(
+                found, sel[...], preferred_element_type=F32
+            ).astype(BF16)
+
+        @pl.when(k < vols)
+        def _():
+            line_copy(k, vol).start()
+
+        return c
+
+    lax.fori_loop(0, vols, render, 0)
+    lines[vol] = picked[vols]
     lax.fori_loop(0, HEADS, embed, 0)
 
     own[1].wait()
     each(1, dps, lambda k: weight_copy(k, (dp + dps - k) % dps).wait_recv())
 
     out_w = weight[:, :, 192:256].reshape(width, HEAD_DIM).astype(F32)
-    mixed = jnp.dot(head_t[...], out_w, precision=HIGHEST, preferred_element_type=F32)
+    mixed = jnp.dot(head_t, out_w, precision=HIGHEST, preferred_element_type=F32)
 
     def forward(j, c):
         whole = weight[...].reshape(width, 256)
@@ -195,12 +263,11 @@
 
     lax.fori_loop(0, HEADS, forward, 0)
 
-    own[2].wait()
     each(1, vols, lambda k: line_copy(k, (vol + vols - k) % vols).wait_recv())
     rendered = lines[0].astype(F32)
     for other in range(1, vols):
         rendered = rendered + lines[other].astype(F32)
-    slices = jnp.dot(rendered.astype(BF16), sel[...], preferred_element_type=F32)
+    slices = rendered
     lane = lax.broadcasted_iota(jnp.int32, (HEADS, 128), 1)
     row = lax.broadcasted_iota(jnp.int32, (HEADS, 128), 0)
     filt = contrast[0].astype(F32)
@@ -215,7 +282,7 @@
         lax.broadcasted_iota(jnp.int32, (HEADS, width), 0) == head, mean_emb[...], 0.0
     )
     logit = lax.dot_general(
-        own_emb, head_t[...], LAST, precision=HIGHEST, preferred_element_type=F32
+        own_emb, head_t, LAST, precision=HIGHEST, preferred_element_type=F32
     )
     logit = logit + lax.dot_general(
         mean_att[...], mixed, LAST, precision=HIGHEST, preferred_element_type=F32
@@ -240,20 +307,25 @@
     for k in range(K):
         pulled = pulled + slope[:, k : k + 1] * mixed[k : k + 1, :]
     pulled = pulled / PATCHES
-    small_send_slope = slope
-    total[...] = jnp.zeros(total.shape, F32)
-
-    for j in range(HEADS):
+
+    def backward(j, c):
         t = triple[j]
         chosen = attention[j].astype(F32)
-        up = jnp.sum(t[:, 128:192].astype(F32) * pulled[j : j + 1, :], axis=1, keepdims=True)
+        up = jnp.sum(
+            t[:, 128:192].astype(F32) * pulled_buf[pl.ds(j, 1), :], axis=1, keepdims=True
+        )
         center = jnp.sum(chosen * up, axis=0, keepdims=True)
         inner = (chosen * (up - center) * HEAD_DIM ** (-0.5)).astype(BF16)
         key_slope = jnp.dot(inner, t[:, 0:64], preferred_element_type=F32)
         query_slope = lax.dot_general(inner, t[:, 64:128], FIRST, preferred_element_type=F32)
-        spread = column[j] * small_send_slope[j : j + 1, :]
-        terms = jnp.concatenate([query_slope, key_slope, spread], axis=1).astype(BF16)
-        total[...] += lax.dot_general(terms, normed[j], FIRST, preferred_element_type=F32)
+        spread = column[j] * slope_buf[pl.ds(j, 1), :]
+        terms = jnp.concatenate([query_slope, key_slope, spread], axis=1)
+        terms_buf[j] = terms.astype(BF16)
+        return c
+
+    pulled_buf[...] = pulled
+    slope_buf[...] = slope
+    lax.fori_loop(0, HEADS, backward, 0)
 
     outer = lax.dot_general(
         slope, mean_att[...], FIRST, precision=HIGHEST, preferred_element_type=F32
@@ -268,34 +340,88 @@
     pooled_t = pooled_t + lax.dot_general(
         outer, out_w, LAST, precision=HIGHEST, preferred_element_type=F32
     )
-    value_t = total[128:136, :]
-    for d in range(dps):
-        part = slice(d * rows, (d + 1) * rows)
-        grad_send[d] = total[0:128, part].T.astype(BF16)
-        fill = [jnp.zeros((HEADS, 64 - rows), F32)] if rows < 64 else []
-        top = jnp.concatenate([value_t[:, part]] + fill + [outer], axis=1)
-        low = jnp.concatenate([mixed] + [pooled_t[:, part]] + fill, axis=1)
-        tile_send[d] = jnp.where(row < 4, top, pltpu.roll(low, 4, 0))
-
-    def grad_copy(k, slot):
-        to = (me + k) % count
-        return copy(
-            grad_send.at[to // vols], grad_recv.at[slot], grad_sems, k, slot, to // vols, to % vols
-        )
-
-    def tile_copy(k, slot):
-        to = (me + k) % count
-        return copy(
-            tile_send.at[to // vols], tile_recv.at[slot], tile_sems, k, slot, to // vols, to % vols
-        )
-
-    each(1, count, lambda k: tile_copy(k, me).start())
-    each(1, count, lambda k: grad_copy(k, me).start())
+    pooled_buf[...] = pooled_t
+
+    chunk = 256 // rows
+    chunks = dps // chunk
+
+    def send(d, v, start):
+        k = (d * vols + v + count - me) % count
+        one = pltpu.make_async_remote_copy(
+            src_ref=grad_send.at[d],
+            dst_ref=grad_recv.at[me],
+            send_sem=grad_sems.at[0, k],
+            recv_sem=grad_sems.at[1, me],
+            device_id=(d, v),
+            device_id_type=MESH,
+        )
+        two = pltpu.make_async_remote_copy(
+            src_ref=tile_send.at[d],
+            dst_ref=tile_recv.at[me],
+            send_sem=tile_sems.at[0, k],
+            recv_sem=tile_sems.at[1, me],
+            device_id=(d, v),
+            device_id_type=MESH,
+        )
+        if start:
+            two.start()
+            one.start()
+        else:
+            two.wait_send()
+            one.wait_send()
+
+    def combine(step_k, c):
+        at = (dp // chunk + chunks // 2 + step_k) % chunks
+        lanes = pl.ds(pl.multiple_of(at * 256, 256), 256)
+        total = lax.dot_general(
+            terms_buf[...].reshape(HEADS * PATCHES, 256),
+            normed[:, :, lanes].reshape(HEADS * PATCHES, 256),
+            FIRST,
+            preferred_element_type=F32,
+        )
+        ours = total[0:128].T.astype(BF16)
+        value_t = total[128:136]
+        pooled_part = pooled_buf[:, lanes]
+        for i in range(chunk):
+            part = slice(i * rows, (i + 1) * rows)
+            d = at * chunk + i
+            grad_send[d] = ours[part]
+            fill = [jnp.zeros((HEADS, 64 - rows), F32)] if rows < 64 else []
+            top = jnp.concatenate([value_t[:, part]] + fill + [outer], axis=1)
+            low = jnp.concatenate([mixed, pooled_part[:, part]] + fill, axis=1)
+            tile_send[d] = jnp.where(row < 4, top, pltpu.roll(low, 4, 0))
+
+        def out(n, c2):
+            d = at * chunk + n // vols
+            v = n % vols
+
+            @pl.when(d * vols + v != me)
+            def _():
+                send(d, v, True)
+
+            return c2
+
+        lax.fori_loop(0, chunk * vols, out, 0)
+        return c
+
+    lax.fori_loop(0, chunks, combine, 0)
     grad_recv[me] = grad_send[dp]
     tile_recv[me] = tile_send[dp]
-    each(1, count, lambda k: tile_copy(k, (me + count - k) % count).wait_recv())
-
-    pooled_sum = jnp.sum(tile_recv[...], axis=0)
+
+    def arrived(k, src, dst, sems):
+        slot = (me + count - k) % count
+        pltpu.make_async_remote_copy(
+            src_ref=src.at[dp],
+            dst_ref=dst.at[slot],
+            send_sem=sems.at[0, k],
+            recv_sem=sems.at[1, slot],
+            device_id=(dp, vol),
+            device_id_type=MESH,
+        ).wait_recv()
+
+    each(1, count, lambda k: arrived(k, tile_send, tile_recv, tile_sems))
+
+    pooled_sum = pltpu.roll(jnp.sum(tile_recv[...], axis=0), 4, 0)
     head_send[...] = pooled_sum
 
     def head_copy(k, slot):
@@ -305,44 +431,48 @@
     each(1, dps, lambda k: head_copy(k, dp).start())
     head_out[dp] = pooled_sum
 
+    head_own = head_wide[pl.ds(pl.multiple_of(dp * rows, rows), rows), 0:8]
     for h in range(HEADS):
-        senders = [
-            (d * vols + v) for d in range(h, dps, HEADS) for v in range(vols)
-        ]
+        senders = [(d * vols + v) for d in range(h, dps, HEADS) for v in range(vols)]
         tile = tile_recv[senders[0]]
         mixed_h = jnp.where(row < 4, pltpu.roll(tile, 4, 0), 0.0)[:, 0:64]
         for s in senders[1:]:
             tile = tile + tile_recv[s]
         tile = jnp.where(row < 4, tile, 0.0)
-        lanes = slice(h * 64, h * 64 + 64)
-        in_out[:, 1024 + h * 64 : 1088 + h * 64] = (
+        value_out[:, h * 64 : h * 64 + 64] = (
             lax.dot_general(
                 tile[:, 0:rows], mixed_h, FIRST, precision=HIGHEST, preferred_element_type=F32
             )
             / PATCHES
         )
-        out_out[:, lanes] = lax.dot_general(
-            head_own[...], tile[:, 64:128], FIRST, precision=HIGHEST, preferred_element_type=F32
-        )
-    each(1, count, lambda k: grad_copy(k, (me + count - k) % count).wait_recv())
-    for h in range(HEADS):
-        senders = [
-            (d * vols + v) for d in range(h, dps, HEADS) for v in range(vols)
-        ]
-        both = grad_recv[senders[0]].astype(F32)
-        for s in senders[1:]:
-            both = both + grad_recv[s].astype(F32)
-        in_out[:, h * 64 : h * 64 + 64] = both[:, 0:64]
-        in_out[:, 512 + h * 64 : 576 + h * 64] = both[:, 64:128]
+        value_out[:, 512 + h * 64 : 576 + h * 64] = jnp.dot(
+            head_own, tile[:, 64:128], precision=HIGHEST, preferred_element_type=F32
+        )
+    each(1, count, lambda k: arrived(k, grad_send, grad_recv, grad_sems))
     each(1, dps, lambda k: head_copy(k, (dp + dps - k) % dps).wait_recv())
 
     each(1, HEADS, lambda k: patch_copy(k, head).wait_send())
     each(1, dps, lambda k: weight_copy(k, dp).wait_send())
     each(1, vols, lambda k: line_copy(k, vol).wait_send())
     each(1, HEADS, lambda k: small_copy(k, head).wait_send())
-    each(1, count, lambda k: tile_copy(k, me).wait_send())
-    each(1, count, lambda k: grad_copy(k, me).wait_send())
+    each(1, count, lambda k: send(((me + k) % count) // vols, (me + k) % vols, False))
     each(1, dps, lambda k: head_copy(k, dp).wait_send())
+
+
+def finish(dps, vols, errors, grads, values, heads, errors_out, in_out, out_out, head_out):
+    rows = values.shape[0]
+    for h in range(HEADS):
+        senders = [(d * vols + v) for d in range(h, dps, HEADS) for v in range(vols)]
+        both = grads[senders[0]].astype(F32)
+        for s in senders[1:]:
+            both = both + grads[s].astype(F32)
+        in_out[:, h * 64 : h * 64 + 64] = both[:, 0:64]
+        in_out[:, 512 + h * 64 : 576 + h * 64] = both[:, 64:128]
+    in_out[:, 1024:1536] = values[:, 0:512]
+    out_out[...] = values[:, 512:1024]
+    errors_out[...] = errors[0:1, 0:K]
+    for d in range(dps):
+        head_out[d * rows : (d + 1) * rows, :] = heads[d].T[64 : 64 + rows, 0:K]
 
 
 def constants():
@@ -352,7 +482,10 @@
     waves = np.stack([cosine, sine, (cosine + sine).T, (cosine - sine).T]).astype(np.float32)
     sel = np.zeros((2 * PIX, PIX), np.float32)
     sel[2 * np.arange(PIX), np.arange(PIX)] = 1.0
-    return waves, sel
+    places = np.zeros((PATCH, PIX, PIX), np.float32)
+    for r in range(PATCH):
+        places[r, np.arange(PIX), r * PATCH + np.arange(PIX) % PATCH] = 1.0
+    return waves, sel, places
 
 
 def local(
@@ -372,38 +505,32 @@
     width = norm_gain.shape[0]
     rows = project_in.shape[0]
     count = dps * vols
-    waves, sel = constants()
+    waves, sel, places = constants()
     slab, side, _ = volume.shape
-    plane = line_index // side - lax.axis_index("vol") * slab
-    inside = (plane >= 0) & (plane < slab)
-    spot = jnp.clip(plane, 0, slab - 1) * side + line_index % side
-    picked = jnp.take(volume.reshape(slab * side, side), spot.reshape(-1), axis=0)
-    picked = jnp.where(inside.reshape(-1, 1), picked, jnp.zeros((), BF16))
-    picked = picked.reshape(vols, K * PIX, side)
-
-    grid = PIX // PATCH
-    patches = images[0].astype(BF16).reshape(2, grid // 2, PATCH, grid, PATCH)
-    patches = patches.transpose(1, 3, 0, 2, 4).reshape(PATCHES // 2, 2 * PATCH * PATCH)
-    parts = project_in.reshape(rows, 3, HEADS, HEAD_DIM).transpose(2, 0, 1, 3)
-    pieces = jnp.concatenate(
-        [parts, project_out.reshape(rows, HEADS, 1, HEAD_DIM).transpose(1, 0, 2, 3)], axis=2
-    ).reshape(HEADS, rows, 4 * HEAD_DIM)
-    head_t = jnp.pad(head_weight.T, ((0, 4), (0, 0)))
-    head_own = lax.dynamic_slice(head_t, (0, lax.axis_index("dp") * rows), (8, rows))
-
     vmem = pl.BlockSpec(memory_space=pltpu.VMEM)
-    errors, in_grad, out_grad, head_grad = pl.pallas_call(
+    errors, grads, values, heads = pl.pallas_call(
         functools.partial(step, dps, vols),
         out_shape=(
             jax.ShapeDtypeStruct((8, 128), F32),
-            jax.ShapeDtypeStruct((rows, 3 * HEADS * HEAD_DIM), F32),
-            jax.ShapeDtypeStruct((rows, HEADS * HEAD_DIM), F32),
+            jax.ShapeDtypeStruct((count, rows, 128), BF16),
+            jax.ShapeDtypeStruct((rows, 1024), F32),
             jax.ShapeDtypeStruct((dps, 8, 128), F32),
         ),
-        in_specs=[vmem] * 12,
+        in_specs=[
+            pl.BlockSpec(memory_space=pltpu.SMEM),
+            vmem,
+            pl.BlockSpec(memory_space=pltpu.HBM),
+        ]
+        + [vmem] * 11,
         out_specs=(vmem,) * 4,
         scratch_shapes=[
-            pltpu.VMEM((vols, K * PIX, side), BF16),
+            pltpu.VMEM((slab, 16, 16, side), BF16),
+            pltpu.VMEM((vols + 1, K * PIX, PIX), BF16),
+            pltpu.VMEM((PATCHES // 2, 128), BF16),
+            pltpu.VMEM((HEADS, rows, 256), BF16),
+            pltpu.VMEM((width, 128), F32),
+            pltpu.VMEM((HEADS, PATCHES, 256), BF16),
+            pltpu.VMEM((vols, K * PIX, PIX), BF16),
             pltpu.VMEM((HEADS, PATCHES // 2, 128), BF16),
             pltpu.VMEM((dps, rows, 256), BF16),
             pltpu.VMEM((HEADS, PATCHES, width), BF16),
@@ -414,10 +541,11 @@
             pltpu.VMEM((HEADS, HEAD_DIM), F32),
             pltpu.VMEM((16, 128), F32),
             pltpu.VMEM((HEADS, 16, 128), F32),
-            pltpu.VMEM((256, width), F32),
+            pltpu.VMEM((HEADS, HEAD_DIM), F32),
+            pltpu.VMEM((HEADS, 128), F32),
+            pltpu.VMEM((HEADS, width), F32),
             pltpu.VMEM((dps, rows, 128), BF16),
             pltpu.VMEM((dps, 8, 128), F32),
-            pltpu.VMEM((count, rows, 128), BF16),
             pltpu.VMEM((count, 8, 128), F32),
             pltpu.VMEM((8, 128), F32),
             pltpu.SemaphoreType.DMA((2, vols)),
@@ -434,21 +562,33 @@
         ),
         name="pose_step",
     )(
-        picked,
-        patches,
-        pieces,
+        line_index,
+        line_index,
+        volume.reshape(slab, side // 16, 16, side),
         images,
         contrast,
         patch_weight,
         position,
         norm_gain.reshape(1, width),
-        head_t,
-        head_own,
+        project_in,
+        project_out,
+        head_weight,
         jnp.asarray(waves),
         jnp.asarray(sel, BF16),
-    )
-    head_grad = head_grad[:, 4:8, 64 : 64 + rows].transpose(0, 2, 1).reshape(width, 4)
-    return errors[0:1, 0:K], in_grad, out_grad, head_grad
+        jnp.asarray(places, BF16),
+    )
+    return pl.pallas_call(
+        functools.partial(finish, dps, vols),
+        out_shape=(
+            jax.ShapeDtypeStruct((1, K), F32),
+            jax.ShapeDtypeStruct((rows, 3 * HEADS * HEAD_DIM), F32),
+            jax.ShapeDtypeStruct((rows, HEADS * HEAD_DIM), F32),
+            jax.ShapeDtypeStruct((width, K), F32),
+        ),
+        in_specs=[vmem] * 4,
+        out_specs=(vmem,) * 4,
+        name="finish",
+    )(errors, grads, values, heads)
 
 
 def solution(mesh):

time: 90.1 us -> 67.7 us (0.75)
  local copies, waits for them, and re-layouts: 25.8 us -> 3.57 us
  Pallas kernels: 58.2 us -> 63.2 us
  other arithmetic: 4.78 us -> 0 us
    gather x1 -> x0, local copies, waits for them, and re-layouts: 11.6 us -> none  [local(): jnp.take(volume.reshape(slab * side, side), spot.reshape(-1), axis=0)]
    reshape x8 -> x0, local copies, waits for them, and re-layouts: 5.23 us -> none  [the longest x2 1.39 us: local(): parts = project_in.reshape(rows, 3, HEADS, HEAD_DIM).transpose(2, 0, 1, 3)]
    pallas_call x1, Pallas kernels: 58.2 us -> 60.8 us  [local(): pl.pallas_call(functools.partial(step, dps, vols), out_shape=(jax.ShapeDt...]
    pallas_call x0 -> x1, Pallas kernels: none -> 2.42 us  [local(): pl.pallas_call(functools.partial(finish, dps, vols), out_shape=(jax.Shape...]
    pallas_call x0 -> x1, local copies, waits for them, and re-layouts: none -> 1.83 us  [local(): pl.pallas_call(functools.partial(finish, dps, vols), out_shape=(jax.Shape...]
    unnamed x3 -> x1, local copies, waits for them, and re-layouts: 3.34 us -> 1.73 us
    unnamed x2 -> x0, other arithmetic: 1.4 us -> none
    dynamic_slice x1 -> x0, local copies, waits for them, and re-layouts: 1.35 us -> none  [local(): lax.dynamic_slice(head_t, (0, lax.axis_index('dp') * rows), (8, rows))]
where the time goes in v2:
time: 67.7 us; the launch traced here: 67.4 us
  Pallas kernels  63.2 us (93%)
  local copies, waits for them, and re-layouts  3.57 us (5%)
    pallas_call x1, Pallas kernels, local(): pl.pallas_call(functools.partial(step, dps, vols), out_shape=(jax.ShapeDt...  60.8 us
    pallas_call x1, Pallas kernels, local(): pl.pallas_call(functools.partial(finish, dps, vols), out_shape=(jax.Shape...  2.42 us
    pallas_call x1, local copies, waits for them, and re-layouts, local(): pl.pallas_call(functools.partial(finish, dps, vols), out_shape=(jax.Shape...  1.83 us
    unnamed x1, local copies, waits for them, and re-layouts  1.73 us

profile of v2, /device:TPU:0, one launch (start us, length us, event | category | flops | bytes accessed | tf_op | source)
XLA Modules:
  0.0 67.4 jit_solution(11962062448822638368)
XLA Ops:
  0.6 1.7 %copy.17.head_weight = f32[1024,4]{1,0:T(8,128)} copy(f32[1024,4]{0,1:T(4,128)} %param.22) | data formatting | bytes 32768 | tf_op args[9]
  2.4 60.8 %pose_step.1 = (f32[8,128]{1,0:T(8,128)}, bf16[32,64,128]{2,1,0:T(8,128)(2,1)}, f32[64,1024]{1,0:T(8,128)}, f32[16,8,128]{2,1,0:T(8,128)}) custom-call(s32[2,4,128]{2,1,0:T(4,128)} %index.1, s32[2,4,128]{2,1,0:T(4,128)} %index.1, bf16[128,16,16,256]{3,2,1,0:T(8,128)(2,1)} %bitcast.2, f32[1,128,128]{2,1,0:T(8,128)} %image.1, bf16[1,128,128]{2,1,0:T(8,128)(2,1)} %contrast.1, ...), custom_call_target="tpu_custom_call" | custom-call | tf_op jit(solution)/shard_map/pose_step/pallas_call | solution.py:511
  63.1 2.4 %finish.1 = (f32[1,4]{1,0:T(1,128)}, f32[64,1536]{1,0:T(8,128)}, f32[64,512]{1,0:T(8,128)}, f32[1024,4]{1,0:T(8,128)}) custom-call(f32[8,128]{1,0:T(8,128)} %get-tuple-element.8.errors, bf16[32,64,128]{2,1,0:T(8,128)(2,1)} %get-tuple-element.9.grads, f32[64,1024]{1,0:T(8,128)} %get-tuple-element.10.values, f32[16,8,128]{2,1,0:T(8,128)} %get-tuple-element.11.heads), custom_call_target="tpu_custom_call" | custom-call | tf_op jit(solution)/shard_map/finish/pallas_call | solution.py:580
  65.5 1.8 %copy.18 = f32[1024,4]{0,1:T(4,128)} copy(f32[1024,4]{1,0:T(8,128)} %get-tuple-element.15) | data formatting | bytes 32768 | tf_op jit(solution)/shard_map/finish/pallas_call | solution.py:580

commit v3 on v2

--- a/solution.py
+++ b/solution.py
@@ -77,6 +77,8 @@
     tile_sems,
     head_sems,
     local_sems,
+    relay_sems,
+    pass_sems,
 ):
     dp = lax.axis_index("dp")
     vol = lax.axis_index("vol")
@@ -147,7 +149,49 @@
         lax.fori_loop(first, last, run, 0)
 
     each(1, HEADS, lambda k: patch_copy(k, head).start())
-    each(1, dps, lambda k: weight_copy(k, dp).start())
+    share = dp % vols == vol
+
+    def weight_start(k, start):
+        to = (dp + k) % dps
+
+        @pl.when(jnp.logical_or(to // HEADS == dp // HEADS, share))
+        def _():
+            if start:
+                weight_copy(k, dp).start()
+            else:
+                weight_copy(k, dp).wait_send()
+
+    each(1, dps, lambda k: weight_start(dps - k, True))
+
+    def weight_relay(n, v_step):
+        s = (base + HEADS + n) % dps
+        return pltpu.make_async_remote_copy(
+            src_ref=weight.at[s],
+            dst_ref=weight.at[s],
+            send_sem=pass_sems.at[n * vols + v_step],
+            recv_sem=weight_sems.at[1, s],
+            device_id=(dp, (vol + v_step) % vols),
+            device_id_type=MESH,
+        )
+
+    def weight_pass(n, start):
+        s = (base + HEADS + n) % dps
+
+        @pl.when(s % vols == vol)
+        def _():
+            if start:
+                weight_copy((dp + dps - s) % dps, s).wait_recv()
+                each(1, vols, lambda v_step: weight_relay(n, v_step).start())
+            else:
+                each(1, vols, lambda v_step: weight_relay(n, v_step).wait_send())
+
+    def weight_rest(k):
+        s = (dp + dps - k) % dps
+
+        @pl.when(jnp.logical_or(s // HEADS == dp // HEADS, s % vols != vol))
+        def _():
+            weight_copy(k, s).wait_recv()
+
     own = [
         pltpu.make_async_copy(patches, patch_buf.at[head], local_sems.at[0]),
         pltpu.make_async_copy(pieces.at[head], weight.at[dp], local_sems.at[1]),
@@ -166,8 +210,11 @@
     )
     spectrum = spectrum / PIX
 
-    head_wide[...] = jnp.concatenate([head_weight[...], jnp.zeros((width, 124), F32)], axis=1)
-    head_t = head_wide[...].T[0:8]
+    head_t = jnp.concatenate([head_weight[...], jnp.zeros((4, width), F32)], axis=0)
+    near = pl.ds(pl.multiple_of(dp * rows // 128 * 128, 128), 128)
+    head_wide[...] = jnp.concatenate(
+        [head_weight[:, near], jnp.zeros((4, 128), F32)], axis=0
+    ).T
 
     own[0].wait()
 
@@ -235,10 +282,12 @@
 
     lax.fori_loop(0, vols, render, 0)
     lines[vol] = picked[vols]
-    lax.fori_loop(0, HEADS, embed, 0)
+    lax.fori_loop(0, 4, embed, 0)
+    each(0, dps - HEADS, lambda n: weight_pass(n, True))
+    lax.fori_loop(4, HEADS, embed, 0)
 
     own[1].wait()
-    each(1, dps, lambda k: weight_copy(k, (dp + dps - k) % dps).wait_recv())
+    each(1, dps, weight_rest)
 
     out_w = weight[:, :, 192:256].reshape(width, HEAD_DIM).astype(F32)
     mixed = jnp.dot(head_t, out_w, precision=HIGHEST, preferred_element_type=F32)
@@ -363,12 +412,18 @@
             device_id=(d, v),
             device_id_type=MESH,
         )
+        near = jnp.logical_or(d // HEADS == dp // HEADS, v == vol)
         if start:
             two.start()
-            one.start()
         else:
             two.wait_send()
-            one.wait_send()
+
+        @pl.when(near)
+        def _():
+            if start:
+                one.start()
+            else:
+                one.wait_send()
 
     def combine(step_k, c):
         at = (dp // chunk + chunks // 2 + step_k) % chunks
@@ -431,7 +486,7 @@
     each(1, dps, lambda k: head_copy(k, dp).start())
     head_out[dp] = pooled_sum
 
-    head_own = head_wide[pl.ds(pl.multiple_of(dp * rows, rows), rows), 0:8]
+    head_own = head_wide[pl.ds(pl.multiple_of(dp * rows % 128, rows), rows), :]
     for h in range(HEADS):
         senders = [(d * vols + v) for d in range(h, dps, HEADS) for v in range(vols)]
         tile = tile_recv[senders[0]]
@@ -448,11 +503,42 @@
         value_out[:, 512 + h * 64 : 576 + h * 64] = jnp.dot(
             head_own, tile[:, 64:128], precision=HIGHEST, preferred_element_type=F32
         )
-    each(1, count, lambda k: arrived(k, grad_send, grad_recv, grad_sems))
+
+    far = dps - HEADS
+
+    def relay(n, v_step):
+        s = (base + HEADS + n) % dps
+        slot = s * vols + vol
+        return pltpu.make_async_remote_copy(
+            src_ref=grad_recv.at[slot],
+            dst_ref=grad_recv.at[slot],
+            send_sem=relay_sems.at[n * vols + v_step],
+            recv_sem=grad_sems.at[1, slot],
+            device_id=(dp, (vol + v_step) % vols),
+            device_id_type=MESH,
+        )
+
+    def pass_on(n):
+        slot = ((base + HEADS + n) % dps) * vols + vol
+        arrived((me + count - slot) % count, grad_send, grad_recv, grad_sems)
+        each(1, vols, lambda v_step: relay(n, v_step).start())
+
+    each(0, far, pass_on)
+
+    def rest(k):
+        slot = (me + count - k) % count
+
+        @pl.when(jnp.logical_or(slot // vols // HEADS == dp // HEADS, slot % vols != vol))
+        def _():
+            arrived(k, grad_send, grad_recv, grad_sems)
+
+    each(1, count, rest)
+    each(0, far, lambda n: each(1, vols, lambda v_step: relay(n, v_step).wait_send()))
     each(1, dps, lambda k: head_copy(k, (dp + dps - k) % dps).wait_recv())
 
     each(1, HEADS, lambda k: patch_copy(k, head).wait_send())
-    each(1, dps, lambda k: weight_copy(k, dp).wait_send())
+    each(1, dps, lambda k: weight_start(dps - k, False))
+    each(0, dps - HEADS, lambda n: weight_pass(n, False))
     each(1, vols, lambda k: line_copy(k, vol).wait_send())
     each(1, HEADS, lambda k: small_copy(k, head).wait_send())
     each(1, count, lambda k: send(((me + k) % count) // vols, (me + k) % vols, False))
@@ -472,7 +558,7 @@
     out_out[...] = values[:, 512:1024]
     errors_out[...] = errors[0:1, 0:K]
     for d in range(dps):
-        head_out[d * rows : (d + 1) * rows, :] = heads[d].T[64 : 64 + rows, 0:K]
+        head_out[:, d * rows : (d + 1) * rows] = heads[d][0:K, 64 : 64 + rows]
 
 
 def constants():
@@ -528,7 +614,7 @@
             pltpu.VMEM((vols + 1, K * PIX, PIX), BF16),
             pltpu.VMEM((PATCHES // 2, 128), BF16),
             pltpu.VMEM((HEADS, rows, 256), BF16),
-            pltpu.VMEM((width, 128), F32),
+            pltpu.VMEM((128, 8), F32),
             pltpu.VMEM((HEADS, PATCHES, 256), BF16),
             pltpu.VMEM((vols, K * PIX, PIX), BF16),
             pltpu.VMEM((HEADS, PATCHES // 2, 128), BF16),
@@ -556,6 +642,8 @@
             pltpu.SemaphoreType.DMA((2, count)),
             pltpu.SemaphoreType.DMA((2, dps)),
             pltpu.SemaphoreType.DMA((3,)),
+            pltpu.SemaphoreType.DMA((dps * vols,)),
+            pltpu.SemaphoreType.DMA((dps * vols,)),
         ],
         compiler_params=pltpu.CompilerParams(
             collective_id=0, has_side_effects=True, vmem_limit_bytes=56 * 1024 * 1024
@@ -572,23 +660,24 @@
         norm_gain.reshape(1, width),
         project_in,
         project_out,
-        head_weight,
+        head_weight.T,
         jnp.asarray(waves),
         jnp.asarray(sel, BF16),
         jnp.asarray(places, BF16),
     )
-    return pl.pallas_call(
+    errors, in_grad, out_grad, head_grad = pl.pallas_call(
         functools.partial(finish, dps, vols),
         out_shape=(
             jax.ShapeDtypeStruct((1, K), F32),
             jax.ShapeDtypeStruct((rows, 3 * HEADS * HEAD_DIM), F32),
             jax.ShapeDtypeStruct((rows, HEADS * HEAD_DIM), F32),
-            jax.ShapeDtypeStruct((width, K), F32),
+            jax.ShapeDtypeStruct((K, width), F32),
         ),
         in_specs=[vmem] * 4,
         out_specs=(vmem,) * 4,
         name="finish",
     )(errors, grads, values, heads)
+    return errors, in_grad, out_grad, head_grad.T
 
 
 def solution(mesh):

time: 67.7 us -> 61.7 us (0.911)
  local copies, waits for them, and re-layouts: 3.57 us -> 0 us
  Pallas kernels: 63.2 us -> 60.9 us
    pallas_call x1, Pallas kernels: 60.8 us -> 58.9 us  [local(): pl.pallas_call(functools.partial(step, dps, vols), out_shape=(jax.ShapeDt...]
    pallas_call x1 -> x0, local copies, waits for them, and re-layouts: 1.83 us -> none  [local(): pl.pallas_call(functools.partial(finish, dps, vols), out_shape=(jax.Shape...]
    unnamed x1 -> x0, local copies, waits for them, and re-layouts: 1.73 us -> none
where the time goes in v3:
time: 61.7 us; the launch traced here: 61.6 us
  Pallas kernels  60.9 us (99%)
  between operations  0.64 us (1%)
    pallas_call x1, Pallas kernels, local(): pl.pallas_call(functools.partial(step, dps, vols), out_shape=(jax.ShapeDt...  58.9 us
    pallas_call x1, Pallas kernels, local(): pl.pallas_call(functools.partial(finish, dps, vols), out_shape=(jax.Shape...  2.05 us

profile of v3, /device:TPU:0, one launch (start us, length us, event | category | flops | bytes accessed | tf_op | source)
XLA Modules:
  0.0 61.6 jit_solution(6192853078652060558)
XLA Ops:
  0.6 58.9 %pose_step.1 = (f32[8,128]{1,0:T(8,128)}, bf16[32,64,128]{2,1,0:T(8,128)(2,1)}, f32[64,1024]{1,0:T(8,128)}, f32[16,8,128]{2,1,0:T(8,128)}) custom-call(s32[2,4,128]{2,1,0:T(4,128)} %index.1, s32[2,4,128]{2,1,0:T(4,128)} %index.1, bf16[128,16,16,256]{3,2,1,0:T(8,128)(2,1)} %bitcast.4, f32[1,128,128]{2,1,0:T(8,128)} %image.1, bf16[1,128,128]{2,1,0:T(8,128)(2,1)} %contrast.1, ...), custom_call_target="tpu_custom_call" | custom-call | tf_op jit(solution)/shard_map/pose_step/pallas_call | solution.py:597
  59.5 2.0 %finish.1 = (f32[1,4]{1,0:T(1,128)}, f32[64,1536]{1,0:T(8,128)}, f32[64,512]{1,0:T(8,128)}, f32[4,1024]{1,0:T(4,128)}) custom-call(f32[8,128]{1,0:T(8,128)} %get-tuple-element.12.errors, bf16[32,64,128]{2,1,0:T(8,128)(2,1)} %get-tuple-element.13.grads, f32[64,1024]{1,0:T(8,128)} %get-tuple-element.14.values, f32[16,8,128]{2,1,0:T(8,128)} %get-tuple-element.15.heads), custom_call_target="tpu_custom_call" | custom-call | tf_op jit(solution)/shard_map/finish/pallas_call | solution.py:668
